TPU v7x, 512 devices: a whole 4x8x8 slice. The times are simulated.
512 devices in a mesh: tm: 8 (over z_hi, core), height: 8 (over x, z_lo), head: 8 (over y).
Axes of the slice: x: 4, y: 8, z: 8 (z_hi: 4, z_lo: 2; z = z_hi * 2 + z_lo), core: 2. Of those that a mesh axis runs over, the one named last changes fastest.
Arguments:
- lat_q: bfloat16 [8, 8, 2, 384, 3072], P('tm', 'height', None, None, 'head'), may hold values from -12 to 12
- lat_kv: bfloat16 [2, 8, 8, 2, 384, 3072], P(None, 'tm', 'height', None, None, 'head'), may hold values from -6 to 6
- txt_qkv: bfloat16 [3, 64, 128, 3072], P(None, ('tm', 'height'), None, 'head'), may hold values from -12 to 12
- blocks: int32 [8, 8, 2, 9], P('tm', 'height'), may hold values from -1 to 127, as said below
- owner: int32 [8], P('head'), may hold values from 0 to 63
Outputs:
- latent_out: bfloat16 [8, 8, 2, 384, 3072], P('tm', 'height', None, None, 'head')
- text_out: bfloat16 [128, 3072], P(None, 'head')
Inputs may be any that keep to these rules, and one draw needn't show every extreme that they name: `blocks`: row i lists its own tile i first, then distinct tiles with the same width index whose frame and height tile indices each differ from tile i's by at most one, then -1 entries; some row lists 9 tiles.
All inputs are finite; a program needn't handle non-finite values.
Results may differ from a plain program's by a relative error of at most 0.0031.
Values may be sent and summed in bfloat16 or wider, within the bound.
No kernel may reach another device: no remote copies, remote signals or barrier semaphores. Data moves between devices by JAX's collectives and lax.ppermute only.
A program may use at most 128 MiB of HBM per device.

v0:
```python
import jax
import jax.numpy as jnp
from jax import lax
from jax.sharding import PartitionSpec as P

HD = 128


def broadcast(value, axis, source):
    kept = jnp.where(lax.axis_index(axis) == source, value, 0).astype(value.dtype)
    return lax.psum(kept, axis)


def padded(x, sides, width):
    for axis, dim in sides:
        count, length = (lax.axis_size(axis), x.shape[dim])
        up = [(i, (i + 1) % count) for i in range(count - 1)]
        down = [(j, i) for i, j in up]
        last = lax.slice_in_dim(x, length - width, length, axis=dim)
        initial = lax.slice_in_dim(x, 0, width, axis=dim)
        before = lax.ppermute(last, axis, up)
        after = lax.ppermute(initial, axis, down)
        x = jnp.concatenate([before, x, after], axis=dim)
    return x


def combined_all(part, axis, combine):
    gathered = jax.tree.map(lambda a: lax.all_gather(a, axis), part)

    def take(source):
        return jax.tree.map(lambda a: lax.dynamic_index_in_dim(a, source, 0, False), gathered)

    return lax.fori_loop(
        1, lax.axis_size(axis), lambda source, state: combine(state, take(source)), take(0)
    )


def combine(first, second):
    max_first, sum_first, acc_first = first
    max_second, sum_second, acc_second = second
    merged_max = jnp.maximum(max_first, max_second)
    factor_first = jnp.exp(max_first - merged_max)
    factor_second = jnp.exp(max_second - merged_max)
    merged_sum = sum_first * factor_first + sum_second * factor_second
    merged_acc = acc_first * factor_first[..., None] + acc_second * factor_second[..., None]
    return (merged_max, merged_sum, merged_acc)


def text_part(head, text_query, key_block, value_block, inv_root):
    head_query = lax.dynamic_slice_in_dim(text_query, head * HD, HD, 1)
    head_key = lax.dynamic_slice_in_dim(key_block, head * HD, HD, 1)
    head_value = lax.dynamic_slice_in_dim(value_block, head * HD, HD, 1)
    scores = (
        jnp.einsum("qd,kd->qk", head_query, head_key, preferred_element_type=jnp.float32) * inv_root
    )
    row_max = jnp.max(scores, axis=1)
    weights = jnp.exp(scores - row_max[:, None])
    weighted = jnp.dot(weights, head_value, precision=lax.Precision.HIGHEST)
    return (row_max, jnp.sum(weights, axis=1), weighted)


def body(lat_q, lat_kv, txt_qkv, blocks, owner):
    column_count = lat_q.shape[-1]
    head_count = column_count // HD
    width_tiles = lat_q.shape[2]
    tile_rows = lat_q.shape[3]
    list_length = blocks.shape[-1]
    text_count = txt_qkv.shape[2]
    inv_root = HD ** (-0.5)
    owner_text = broadcast(txt_qkv, ("tm", "height"), owner[0])
    text_query = owner_text[0, 0]
    text_key = owner_text[1, 0]
    text_value = owner_text[2, 0]
    extended = padded(lat_kv, (("tm", 1), ("height", 2)), 1)
    near_keys = extended[0].reshape(9 * width_tiles, tile_rows, column_count)
    near_values = extended[1].reshape(9 * width_tiles, tile_rows, column_count)
    my_time = lax.axis_index("tm")
    my_height = lax.axis_index("height")
    height_count = lax.axis_size("height")
    tile_outputs = []
    for width_index in range(width_tiles):
        tile_ids = blocks[0, 0, width_index]
        listed = tile_ids >= 0
        clamped = jnp.maximum(tile_ids, 0)
        key_time = clamped // (height_count * width_tiles)
        key_height = clamped // width_tiles % height_count
        key_width = clamped % width_tiles
        position = (
            (key_time - my_time + 1) * 3 + (key_height - my_height + 1)
        ) * width_tiles + key_width
        position = jnp.where(listed, position, 0)
        key_rows = jnp.concatenate(
            [near_keys[position].reshape(list_length * tile_rows, column_count), text_key], 0
        )
        value_rows = jnp.concatenate(
            [near_values[position].reshape(list_length * tile_rows, column_count), text_value], 0
        )
        key_bias = jnp.concatenate(
            [
                jnp.repeat(jnp.where(listed, 0.0, -1e30).astype(jnp.float32), tile_rows),
                jnp.zeros((text_count,), jnp.float32),
            ]
        )
        queries = lat_q[0, 0, width_index]

        def one_head(head):
            head_query = lax.dynamic_slice_in_dim(queries, head * HD, HD, 1)
            head_key = lax.dynamic_slice_in_dim(key_rows, head * HD, HD, 1)
            head_value = lax.dynamic_slice_in_dim(value_rows, head * HD, HD, 1)
            scores = (
                jnp.einsum("qd,kd->qk", head_query, head_key, preferred_element_type=jnp.float32)
                * inv_root
                + key_bias[None, :]
            )
            row_max = jnp.max(scores, axis=1, keepdims=True)
            weights = jnp.exp(scores - row_max)
            row_sum = jnp.sum(weights, axis=1, keepdims=True)
            mixed = (
                jnp.dot(
                    weights.astype(jnp.bfloat16), head_value, preferred_element_type=jnp.float32
                )
                / row_sum
            )
            return mixed.astype(jnp.bfloat16)

        per_head = lax.map(one_head, jnp.arange(head_count, dtype=jnp.int32))
        tile_outputs.append(jnp.transpose(per_head, (1, 0, 2)).reshape(tile_rows, column_count))
    latent_out = jnp.stack(tile_outputs)[None, None]
    own_keys = lat_kv[0, 0, 0].reshape(width_tiles * tile_rows, column_count)
    own_values = lat_kv[1, 0, 0].reshape(width_tiles * tile_rows, column_count).astype(jnp.float32)

    def partial_head(head):
        return text_part(head, text_query, own_keys, own_values, inv_root)

    part_max, part_sum, part_acc = lax.map(partial_head, jnp.arange(head_count, dtype=jnp.int32))
    part_max, part_sum, part_acc = combined_all(
        (part_max, part_sum, part_acc), ("tm", "height"), combine
    )
    text_value_wide = text_value.astype(jnp.float32)

    def text_head(head):
        return text_part(head, text_query, text_key, text_value_wide, inv_root)

    own_text = lax.map(text_head, jnp.arange(head_count, dtype=jnp.int32))
    final_max, final_sum, final_acc = combine((part_max, part_sum, part_acc), own_text)
    text_mixed = final_acc / final_sum[..., None]
    text_out = (
        jnp.transpose(text_mixed, (1, 0, 2)).reshape(text_count, column_count).astype(jnp.bfloat16)
    )
    return (latent_out, text_out)


def solution(mesh):
    placed = (
        P("tm", "height", None, None, "head"),
        P(None, "tm", "height", None, None, "head"),
        P(None, ("tm", "height"), None, "head"),
        P("tm", "height", None, None),
        P("head"),
    )
    return jax.shard_map(
        body,
        mesh=mesh,
        in_specs=placed,
        out_specs=(P("tm", "height", None, None, "head"), P(None, "head")),
        check_vma=False,
    )
```

profile of v0, /device:TPU:256, one launch (start us, length us, event | category | flops | bytes accessed | tf_op | source)
XLA Modules:
  0.0 952.4 jit_solution(2615295721121671516)
XLA Ops:
  8.7 1.4 fusion.88
  10.2 190.5 %all-reduce.4.cloned.1.call-done = bf16[3,1,128,384]{3,2,1,0:T(8,128)(2,1)} async-done(((bf16[3,1,128,384]{3,2,1,0:T(8,128)(2,1)}), bf16[3,1,128,384]{3,2,1,0:T(8,128)(2,1)}) %all-reduce.4.cloned.1.call-update) | async-done | bytes 294928 | tf_op jit(solution)/shard_map/psum | solution.py:11
  200.7 1.7 fusion.79
  202.5 9.2 while.69
  211.7 1.9 collective-permute-start
  213.6 5.8 collective-permute-start.1
  219.4 21.7 %collective-permute-done = bf16[2,1,1,2,384,384]{5,4,3,2,1,0:T(8,128)(2,1)S(1)} collective-permute-done((bf16[2,1,1,2,384,384]{5,4,3,2,1,0:T(8,128)(2,1)}, bf16[2,1,1,2,384,384]{5,4,3,2,1,0:T(8,128)(2,1)S(1)}, u32[]{:S(2)}, u32[]{:S(2)}) %collective-permute-start) | collective-permute-done | bytes 1179680 | tf_op jit(solution)/shard_map/ppermute | solution.py:21
  241.3 1.5 constant_dynamic-update-slice_fusion.3
  242.8 10.3 %collective-permute-done.1 = bf16[2,1,1,2,384,384]{5,4,3,2,1,0:T(8,128)(2,1)S(1)} collective-permute-done((bf16[2,1,1,2,384,384]{5,4,3,2,1,0:T(8,128)(2,1)}, bf16[2,1,1,2,384,384]{5,4,3,2,1,0:T(8,128)(2,1)S(1)}, u32[]{:S(2)}, u32[]{:S(2)}) %collective-permute-start.1) | collective-permute-done | bytes 1179680 | tf_op jit(solution)/shard_map/ppermute | solution.py:22
  253.4 3.1 collective-permute-start.2
  256.4 1.3 collective-permute-start.3
  260.9 1.3 reshape.383
  265.6 1.9 slice_bitcast_fusion.1
  267.5 279.3 %all-gather.4 = f32[64,3,128]{2,1,0:T(4,128)S(1)} all-gather(f32[1,3,128]{2,1,0:T(4,128)} %bitcast.216), channel_id=3, replica_groups=mesh['tm'=8,'height'=8,'head'=8] {'tm','height'}, dimensions={0}, use_global_device_ids=true | all-gather | bytes 99840 | tf_op jit(solution)/shard_map/all_gather | solution.py:28
  546.8 124.9 %all-gather.3 = f32[64,3,128]{2,1,0:T(4,128)S(1)} all-gather(f32[1,3,128]{2,1,0:T(4,128)} %bitcast.215), channel_id=2, replica_groups=mesh['tm'=8,'height'=8,'head'=8] {'tm','height'}, dimensions={0}, use_global_device_ids=true | all-gather | bytes 99840 | tf_op jit(solution)/shard_map/all_gather | solution.py:28
  674.6 23.0 %while.71 = (s32[]{:T(128)}, f32[3,128]{1,0:T(4,128)}, f32[3,128]{1,0:T(4,128)}, f32[3,128,128]{1,2,0:T(8,128)}, s32[3]{0:T(128)}, /*index=5*/bf16[128,384]{1,0:...) while((s32[]{:T(128)}, f32[3,128]{1,0:T(4,128)}, ...), condition=%wide.region_18.19_spmd, body=%wide.region_15.18_spmd.sunk | while | flops 29441796 | bytes 401111 | solution.py:144
  677.4 1.8 fusion.128
  685.1 1.8 fusion.128
  692.8 1.8 fusion.128
  697.6 8.3 pad_maximum_fusion
  705.9 9.8 %fusion.87 = (bf16[1,3,3,2,384,384]{5,4,3,2,1,0:T(8,128)(2,1)}, bf16[1,3,3,2,384,384]{5,4,3,2,1,0:T(8,128)(2,1)}) fusion(bf16[2,3,3,2,384,384]{5,4,3,2,1,0:T(8,128)(2,1)} %pad_maximum_fusion), kind=kLoop, calls=%fused_computation.133 | loop fusion | bytes 21233664 | tf_op jit(solution)/shard_map/slice | solution.py:76
  715.6 5.4 gather_fusion.1
  721.0 5.3 gather_fusion.3
  726.3 5.4 gather_fusion.2
  731.7 5.3 gather_fusion
  737.1 10.2 %pad_maximum_fusion.2 = (bf16[3584,384]{1,0:T(8,128)(2,1)}, bf16[3584,384]{1,0:T(8,128)(2,1)S(1)}, bf16[3584,384]{1,0:T(8,128)(2,1)}, bf16[3584,384]{1,0:T(8,128)(2,1)}) fusion(bf16[128,384]{1,0:T(8,128)(2,1)S(1)} %copy-done.2, bf16[3456,384]{1,0:T(8,128)(2,1)} %bitcast.205, bf16[3456,384]{1,0:T(8,128)(2,1)} %bitcast.204, bf16[128,384]{1,0:T(8,128)(2,1)S(1)} %copy-done.3, ...), kind=kLoop, calls=%fused_computation.68 | loop fusion | flops 19267584 | bytes 21823488 | tf_op jit(solution)/shard_map/concatenate | solution.py:92
  747.3 20.0 %while.67 = (s32[]{:T(128)}, bf16[3,384,128]{1,2,0:T(8,128)(2,1)S(1)}, s32[3]{0:T(128)S(1)}, bf16[384,384]{1,0:T(8,128)(2,1)}, bf16[3584,384]{1,0:T(8,128)(2,1)}...) while((s32[]{:T(128)}, ...), condition=%wide.region_4.5_spmd, body=%wide.region_1.4_spmd.sunk | while | flops 714374400 | bytes 18963120 | solution.py:126
  748.6 2.2 fusion.111
  751.7 2.1 fusion.113
  755.2 2.2 fusion.111
  758.4 2.1 fusion.113
  761.9 2.3 fusion.111
  765.0 2.1 fusion.113
  767.9 21.2 %while.68 = (s32[]{:T(128)}, bf16[3,384,128]{1,2,0:T(8,128)(2,1)S(1)}, s32[3]{0:T(128)}, bf16[384,384]{1,0:T(8,128)(2,1)}, bf16[3584,384]{1,0:T(8,128)(2,1)S(1)}...) while((s32[]{:T(128)}, ...), condition=%wide.region_8.9_spmd, body=%wide.region_5.8_spmd.sunk | while | flops 714374400 | bytes 18965168 | solution.py:126
  770.0 1.9 fusion.116
  772.8 2.1 fusion.118
  777.0 1.9 fusion.116
  779.8 2.1 fusion.118
  784.0 1.9 fusion.116
  786.8 2.1 fusion.118
  791.2 152.8 %while.70 = (s32[]{:T(128)}, f32[3,128]{1,0:T(4,128)}, f32[3,128]{1,0:T(4,128)}, f32[3,128,128]{2,1,0:T(8,128)S(1)}, f32[64,3,128]{2,1,0:T(4,128)}, /*index=5*/f...) while((s32[]{:T(128)}, f32[3,128]{1,0:T(4,128)}, ...), condition=%wide.region_14.15_spmd, body=%wide.region_13.14_spmd.sunk | while | flops 149765 | bytes 605335 | solution.py:33
  791.2 1.3 fusion.123
  822.7 1.3 fusion.123
  847.0 1.3 fusion.123
  859.1 1.3 fusion.123
  883.3 1.3 fusion.123
  895.4 1.3 fusion.123
  914.8 1.3 fusion.123
  (247 shorter events, 191.9 us)
Async XLA Ops:
  7.2 193.6 %all-reduce.4.cloned.1.call-start = ((), (), s32[]{:S(2)}) async-start(), calls=%async_computation | async-start | bytes 589824 | tf_op jit(solution)/shard_map/psum | solution.py:11
  8.6 781.6 %all-gather.7.cloned.1.call-start = ((), (), s32[]{:S(2)}) async-start(), calls=%async_computation.1 | async-start | bytes 12779520 | tf_op jit(solution)/shard_map/all_gather | solution.py:28
  211.6 7.8 copy-start.1
  211.6 7.8 copy-start.8
  211.6 7.8 copy-start.9
  211.7 46.0 %copy-start.12 = (s32[1,1,2,9]{3,2,1,0:T(2,128)S(1)}, s32[1,1,2,9]{3,2,1,0:T(2,128)}, u32[]{:S(2)}) copy-start(s32[1,1,2,9]{3,2,1,0:T(2,128)} %param.18) | copy-start | bytes 220
  211.7 29.4 %collective-permute-start = (bf16[2,1,1,2,384,384]{5,4,3,2,1,0:T(8,128)(2,1)}, bf16[2,1,1,2,384,384]{5,4,3,2,1,0:T(8,128)(2,1)S(1)}, u32[]{:S(2)}, u32[]{:S(2)}) collective-permute-start(bf16[2,1,1,2,384,384]{5,4,3,2,1,0:T(8,128)(2,1)} %param.16), channel_id=1, source_target_pairs={{0,64},{64,128},{128,192},{192,256},{256,320},{320,384},{384,448},... | collective-permute-start | bytes 3538952 | tf_op jit(solution)/shard_map/ppermute | solution.py:21
  213.6 39.5 %collective-permute-start.1 = (bf16[2,1,1,2,384,384]{5,4,3,2,1,0:T(8,128)(2,1)}, bf16[2,1,1,2,384,384]{5,4,3,2,1,0:T(8,128)(2,1)S(1)}, u32[]{:S(2)}, u32[]{:S(2)}) collective-permute-start(bf16[2,1,1,2,384,384]{5,4,3,2,1,0:T(8,128)(2,1)} %param.16), channel_id=1, source_target_pairs={{64,0},{128,64},{192,128},{256,192},{320,256},{384,320},{448,384},... | collective-permute-start | bytes 3538952 | tf_op jit(solution)/shard_map/ppermute | solution.py:22
  253.4 444.2 %collective-permute-start.2 = (bf16[2,3,1,2,384,384]{5,4,3,2,1,0:T(8,128)(2,1)S(1)}, bf16[2,3,1,2,384,384]{5,4,3,2,1,0:T(8,128)(2,1)}, u32[]{:S(2)}, u32[]{:S(2)}) collective-permute-start(bf16[2,3,1,2,384,384]{5,4,3,2,1,0:T(8,128)(2,1)S(1)} %constant_dynamic-update-slice_fusion.2), channel_id=1, source_target_pairs={{0,8},{8,16},{16,24},{24,32},{32,40},{40,48},{48,56},{1,9},{9,17},... | collective-permute-start | bytes 10616840 | tf_op jit(solution)/shard_map/ppermute | solution.py:21
  256.4 441.2 %collective-permute-start.3 = (bf16[2,3,1,2,384,384]{5,4,3,2,1,0:T(8,128)(2,1)S(1)}, bf16[2,3,1,2,384,384]{5,4,3,2,1,0:T(8,128)(2,1)}, u32[]{:S(2)}, u32[]{:S(2)}) collective-permute-start(bf16[2,3,1,2,384,384]{5,4,3,2,1,0:T(8,128)(2,1)S(1)} %constant_dynamic-update-slice_fusion.2), channel_id=1, source_target_pairs={{8,0},{16,8},{24,16},{32,24},{40,32},{48,40},{56,48},{9,1},{17,9},... | collective-permute-start | bytes 10616840 | tf_op jit(solution)/shard_map/ppermute | solution.py:22
  546.8 124.9 %copy-start.6 = (f32[64,3,128]{2,1,0:T(4,128)}, f32[64,3,128]{2,1,0:T(4,128)S(1)}, u32[]{:S(2)}) copy-start(f32[64,3,128]{2,1,0:T(4,128)S(1)} %all-gather.4) | copy-start | bytes 294916
  671.7 0.7 copy-start.7
  677.4 2.3 copy-start.4
  685.1 2.3 copy-start.4
  692.8 2.3 copy-start.4
  731.7 5.3 copy-start.2
  731.7 5.3 copy-start.3
  737.1 10.2 %copy-start = (f32[3584]{0:T(1024)S(1)}, f32[3584]{0:T(1024)}, u32[]{:S(2)}) copy-start(f32[3584]{0:T(1024)} %concatenate.27) | copy-start | bytes 43012
  789.1 155.0 %copy-start.10 = (f32[3,128]{1,0:T(4,128)S(1)}, f32[3,128]{1,0:T(4,128)}, u32[]{:S(2)}) copy-start(f32[3,128]{1,0:T(4,128)} %get-tuple-element.349) | copy-start | bytes 4612
  789.1 155.0 %copy-start.11 = (f32[3,128]{1,0:T(4,128)S(1)}, f32[3,128]{1,0:T(4,128)}, u32[]{:S(2)}) copy-start(f32[3,128]{1,0:T(4,128)} %get-tuple-element.352) | copy-start | bytes 4612
  789.1 155.7 %copy-start.5 = (f32[3,128,128]{1,2,0:T(8,128)S(1)}, f32[3,128,128]{1,2,0:T(8,128)}, u32[]{:S(2)}) copy-start(f32[3,128,128]{1,2,0:T(8,128)} %get-tuple-element.350) | copy-start | bytes 589828
Sparse Core Ops, SparseCore 0:
  12.0 188.6 all-reduce.3
  211.8 321.7 all-gather.6
where the time goes:
time: 958 us; the launch traced here: 952 us
  blocking collectives  404 us (42%)
  waiting for transfers between devices  223 us (23%)
  other arithmetic  183 us (19%)
  local copies, waits for them, and re-layouts  67.8 us (7%)
  matrix products  37.9 us (4%)
  between operations  14.9 us (2%)
  starting transfers between devices  12.1 us (1%)
  loops' own time  9.84 us (1%)
    all_gather x2, blocking collectives, combined_all(): gathered = jax.tree.map(lambda a: lax.all_gather(a, axis), part)  404 us
    psum x1, waiting for transfers between devices, broadcast(): return lax.psum(kept, axis)  191 us
    add x64, other arithmetic, combine(): merged_sum = sum_first * factor_first + sum_second * factor_second  80.8 us
    add x63, other arithmetic, combine(): acc_first * factor_first[..., None] + acc_second * factor_second[..., None]  71.1 us
    ppermute x2, waiting for transfers between devices, padded(): before = lax.ppermute(last, axis, up)  21.7 us
  transfers between devices with their start and end apart: 6, of which 3 were waited for; matrix products, arithmetic and copies ran while one was open for 13% of the time, Pallas kernels for 0%

commit v1 on v0

--- a/solution.py
+++ b/solution.py
@@ -6,9 +6,15 @@
 HD = 128
 
 
+def lay_copies(message, axis_key):
+    carry = lax.all_gather(message, axis_key)
+    raw_out = jnp.sum(carry, 0)
+    return raw_out
+
+
 def broadcast(value, axis, source):
     kept = jnp.where(lax.axis_index(axis) == source, value, 0).astype(value.dtype)
-    return lax.psum(kept, axis)
+    return lay_copies(kept, axis)
 
 
 def padded(x, sides, width):

time: 958 us -> 896 us (0.935)
  waiting for transfers between devices: 223 us -> 407 us
  blocking collectives: 404 us -> 247 us
  other arithmetic: 183 us -> 111 us
  local copies, waits for them, and re-layouts: 67.8 us -> 54 us
    all_gather x0 -> x1, waiting for transfers between devices: none -> 213 us  [lay_copies(): carry = lax.all_gather(message, axis_key)]
    psum x1 -> x0, waiting for transfers between devices: 191 us -> none  [broadcast(): return lax.psum(kept, axis)]
    all_gather x2, blocking collectives: 404 us -> 247 us  [combined_all(): gathered = jax.tree.map(lambda a: lax.all_gather(a, axis), part)]
    ppermute x2, waiting for transfers between devices: 10.3 us -> 94.9 us  [padded(): after = lax.ppermute(initial, axis, down)]
    add x64, other arithmetic: 80.8 us -> 1.64 us  [combine(): merged_sum = sum_first * factor_first + sum_second * factor_second]
    ppermute x2, waiting for transfers between devices: 21.7 us -> 98.6 us  [padded(): before = lax.ppermute(last, axis, up)]
  transfers between devices with their start and end apart: 6 -> 6, of which waited for: 3 -> 5; matrix products, arithmetic and copies ran while one was open for 13% -> 12% of each run, Pallas kernels for 0% -> 0%
where the time goes in v1:
time: 896 us; the launch traced here: 893 us
  waiting for transfers between devices  407 us (45%)
  blocking collectives  247 us (28%)
  other arithmetic  111 us (12%)
  local copies, waits for them, and re-layouts  54 us (6%)
  matrix products  37.9 us (4%)
  between operations  14.9 us (2%)
  starting transfers between devices  12.3 us (1%)
  loops' own time  9.9 us (1%)
    all_gather x2, blocking collectives, combined_all(): gathered = jax.tree.map(lambda a: lax.all_gather(a, axis), part)  247 us
    all_gather x1, waiting for transfers between devices, lay_copies(): carry = lax.all_gather(message, axis_key)  213 us
    ppermute x2, waiting for transfers between devices, padded(): before = lax.ppermute(last, axis, up)  98.6 us
    ppermute x2, waiting for transfers between devices, padded(): after = lax.ppermute(initial, axis, down)  94.9 us
    add x63, other arithmetic, combine(): acc_first * factor_first[..., None] + acc_second * factor_second[..., None]  71.5 us
  transfers between devices with their start and end apart: 6, of which 5 were waited for; matrix products, arithmetic and copies ran while one was open for 12% of the time, Pallas kernels for 0%

profile of v1, /device:TPU:256, one launch (start us, length us, event | category | flops | bytes accessed | tf_op | source)
XLA Modules:
  0.0 892.7 jit_solution(5486430429187656467)
XLA Ops:
  8.7 1.4 fusion.88
  10.2 213.0 %all-gather.9.cloned.1.call-done = bf16[192,1,128,384]{3,2,1,0:T(8,128)(2,1)} async-done(((bf16[3,1,128,384]{3,2,1,0:T(8,128)(2,1)}), bf16[192,1,128,384]{3,2,1,0:T(8,128)(2,1)}) %all-gather.9.cloned.1.call-update) | async-done | bytes 18874384 | tf_op jit(solution)/shard_map/all_gather | solution.py:10
  223.2 7.6 bitcast_reduce_fusion
  231.6 9.1 %while.69 = (s32[]{:T(128)}, f32[3,128]{1,0:T(4,128)S(1)}, f32[3,128]{1,0:T(4,128)S(1)}, f32[3,128,128]{2,1,0:T(8,128)}, s32[3]{0:T(128)S(1)}, /*index=5*/bf16[1...) while((s32[]{:T(128)}, f32[3,128]{1,0:T(4,128)S(1)}, ...), condition=%wide.region_12.13_spmd, body=%wide.region_9.12_spmd.sunk | while | flops 176652032 | bytes 1873595 | solution.py:141
  233.1 1.2 fusion.122
  236.2 1.2 fusion.122
  239.2 1.2 fusion.122
  240.8 2.5 collective-permute-start
  243.3 5.2 collective-permute-start.1
  248.5 21.0 %collective-permute-done = bf16[2,1,1,2,384,384]{5,4,3,2,1,0:T(8,128)(2,1)S(1)} collective-permute-done((bf16[2,1,1,2,384,384]{5,4,3,2,1,0:T(8,128)(2,1)}, bf16[2,1,1,2,384,384]{5,4,3,2,1,0:T(8,128)(2,1)S(1)}, u32[]{:S(2)}, u32[]{:S(2)}) %collective-permute-start) | collective-permute-done | bytes 1179680 | tf_op jit(solution)/shard_map/ppermute | solution.py:27
  269.6 1.5 constant_dynamic-update-slice_fusion.3
  271.2 11.4 %collective-permute-done.1 = bf16[2,1,1,2,384,384]{5,4,3,2,1,0:T(8,128)(2,1)S(1)} collective-permute-done((bf16[2,1,1,2,384,384]{5,4,3,2,1,0:T(8,128)(2,1)}, bf16[2,1,1,2,384,384]{5,4,3,2,1,0:T(8,128)(2,1)S(1)}, u32[]{:S(2)}, u32[]{:S(2)}) %collective-permute-start.1) | collective-permute-done | bytes 1179680 | tf_op jit(solution)/shard_map/ppermute | solution.py:28
  282.8 3.1 collective-permute-start.2
  285.9 1.5 collective-permute-start.3
  289.3 1.3 broadcast_in_dim.78
  290.6 1.3 reshape.390
  295.2 1.9 slice_bitcast_fusion.1
  297.1 77.6 %collective-permute-done.2 = bf16[2,3,1,2,384,384]{5,4,3,2,1,0:T(8,128)(2,1)} collective-permute-done((bf16[2,3,1,2,384,384]{5,4,3,2,1,0:T(8,128)(2,1)S(1)}, bf16[2,3,1,2,384,384]{5,4,3,2,1,0:T(8,128)(2,1)}, u32[]{:S(2)}, u32[]{:S(2)}) %collective-permute-start.2) | collective-permute-done | bytes 3538976 | tf_op jit(solution)/shard_map/ppermute | solution.py:27
  374.8 83.5 %collective-permute-done.3 = bf16[2,3,1,2,384,384]{5,4,3,2,1,0:T(8,128)(2,1)} collective-permute-done((bf16[2,3,1,2,384,384]{5,4,3,2,1,0:T(8,128)(2,1)S(1)}, bf16[2,3,1,2,384,384]{5,4,3,2,1,0:T(8,128)(2,1)}, u32[]{:S(2)}, u32[]{:S(2)}) %collective-permute-start.3) | collective-permute-done | bytes 3538976 | tf_op jit(solution)/shard_map/ppermute | solution.py:28
  458.2 8.3 pad_maximum_fusion
  466.5 9.8 %fusion.87 = (bf16[1,3,3,2,384,384]{5,4,3,2,1,0:T(8,128)(2,1)}, bf16[1,3,3,2,384,384]{5,4,3,2,1,0:T(8,128)(2,1)}) fusion(bf16[2,3,3,2,384,384]{5,4,3,2,1,0:T(8,128)(2,1)} %pad_maximum_fusion), kind=kLoop, calls=%fused_computation.134 | loop fusion | bytes 21233664 | tf_op jit(solution)/shard_map/slice | solution.py:82
  476.3 5.5 gather_fusion.1
  481.7 5.3 gather_fusion.3
  487.1 5.4 gather_fusion.2
  492.5 5.4 gather_fusion
  497.9 10.3 %pad_maximum_fusion.2 = (bf16[3584,384]{1,0:T(8,128)(2,1)}, bf16[3584,384]{1,0:T(8,128)(2,1)S(1)}, bf16[3584,384]{1,0:T(8,128)(2,1)}, bf16[3584,384]{1,0:T(8,128)(2,1)}) fusion(bf16[128,384]{1,0:T(8,128)(2,1)S(1)} %copy-done.2, bf16[3456,384]{1,0:T(8,128)(2,1)} %bitcast.209, bf16[3456,384]{1,0:T(8,128)(2,1)} %bitcast.208, bf16[128,384]{1,0:T(8,128)(2,1)S(1)} %copy-done.4, ...), kind=kLoop, calls=%fused_computation.69 | loop fusion | flops 19267584 | bytes 21823488 | tf_op jit(solution)/shard_map/concatenate | solution.py:98
  508.2 20.0 %while.67 = (s32[]{:T(128)}, bf16[3,384,128]{1,2,0:T(8,128)(2,1)S(1)}, s32[3]{0:T(128)S(1)}, bf16[384,384]{1,0:T(8,128)(2,1)}, bf16[3584,384]{1,0:T(8,128)(2,1)}...) while((s32[]{:T(128)}, ...), condition=%wide.region_4.5_spmd, body=%wide.region_1.4_spmd.sunk | while | flops 714374400 | bytes 18963120 | solution.py:132
  509.5 2.3 fusion.111
  512.6 2.1 fusion.113
  516.1 2.3 fusion.111
  519.3 2.1 fusion.113
  522.8 2.3 fusion.111
  526.0 2.1 fusion.113
  529.0 19.2 %while.68 = (s32[]{:T(128)}, bf16[3,384,128]{1,2,0:T(8,128)(2,1)S(1)}, s32[3]{0:T(128)S(1)}, bf16[384,384]{1,0:T(8,128)(2,1)}, bf16[3584,384]{1,0:T(8,128)(2,1)S...) while((s32[]{:T(128)}, ...), condition=%wide.region_8.9_spmd, body=%wide.region_5.8_spmd.sunk | while | flops 714374400 | bytes 18965168 | solution.py:132
  530.5 1.9 fusion.116
  533.3 2.1 fusion.118
  536.8 1.9 fusion.116
  539.6 2.1 fusion.118
  543.2 1.9 fusion.116
  546.0 2.1 fusion.118
  550.4 122.2 %all-gather.5 = f32[64,3,128]{2,1,0:T(4,128)S(1)} all-gather(f32[1,3,128]{2,1,0:T(4,128)S(1)} %bitcast.220), channel_id=4, replica_groups=mesh['tm'=8,'height'=8,'head'=8] {'tm','height'}, dimensions={0}, use_global_device_ids=true | all-gather | bytes 99840 | tf_op jit(solution)/shard_map/all_gather | solution.py:34
  672.6 124.4 %all-gather.4 = f32[64,3,128]{2,1,0:T(4,128)S(1)} all-gather(f32[1,3,128]{2,1,0:T(4,128)S(1)} %bitcast.219), channel_id=3, replica_groups=mesh['tm'=8,'height'=8,'head'=8] {'tm','height'}, dimensions={0}, use_global_device_ids=true | all-gather | bytes 99840 | tf_op jit(solution)/shard_map/all_gather | solution.py:34
  797.0 12.2 %while.71 = (s32[]{:T(128)}, f32[3,128]{1,0:T(4,128)S(1)}, f32[3,128]{1,0:T(4,128)S(1)}, f32[3,128,128]{1,2,0:T(8,128)}, s32[3]{0:T(128)S(1)}, /*index=5*/bf16[1...) while((s32[]{:T(128)}, f32[3,128]{1,0:T(4,128)S(1)}, ...), condition=%wide.region_18.19_spmd, body=%wide.region_15.18_spmd.sunk | while | flops 29441796 | bytes 399035 | solution.py:150
  799.2 1.8 fusion.128
  803.3 1.8 fusion.128
  807.3 1.8 fusion.128
  810.2 74.7 %while.70 = (s32[]{:T(128)}, f32[3,128]{1,0:T(4,128)S(1)}, f32[3,128]{1,0:T(4,128)S(1)}, f32[3,128,128]{2,1,0:T(8,128)S(1)}, f32[64,3,128]{2,1,0:T(4,128)S(1)}, ...) while((s32[]{:T(128)}, f32[3,128]{1,0:T(4,128)S(1)}, ...), condition=%wide.region_14.15_spmd, body=%wide.region_13.14_spmd.sunk | while | flops 149765 | bytes 605335 | solution.py:39
  810.3 1.1 fusion.124
  (240 shorter events, 102.3 us)
Async XLA Ops:
  7.2 216.0 %all-gather.9.cloned.1.call-start = ((), (), s32[]{:S(2)}) async-start(), calls=%async_computation | async-start | bytes 19169280 | tf_op jit(solution)/shard_map/all_gather | solution.py:10
  8.6 800.6 %all-gather.11.cloned.1.call-start = ((), (), s32[]{:S(2)}) async-start(), calls=%async_computation.1 | async-start | bytes 12779520 | tf_op jit(solution)/shard_map/all_gather | solution.py:34
  240.7 7.8 copy-start.1
  240.7 7.8 copy-start.6
  240.7 7.8 copy-start.8
  240.8 46.6 %copy-start.10 = (s32[1,1,2,9]{3,2,1,0:T(2,128)S(1)}, s32[1,1,2,9]{3,2,1,0:T(2,128)}, u32[]{:S(2)}) copy-start(s32[1,1,2,9]{3,2,1,0:T(2,128)} %param.18) | copy-start | bytes 220
  240.8 28.7 %collective-permute-start = (bf16[2,1,1,2,384,384]{5,4,3,2,1,0:T(8,128)(2,1)}, bf16[2,1,1,2,384,384]{5,4,3,2,1,0:T(8,128)(2,1)S(1)}, u32[]{:S(2)}, u32[]{:S(2)}) collective-permute-start(bf16[2,1,1,2,384,384]{5,4,3,2,1,0:T(8,128)(2,1)} %param.16), channel_id=1, source_target_pairs={{0,64},{64,128},{128,192},{192,256},{256,320},{320,384},{384,448},... | collective-permute-start | bytes 3538952 | tf_op jit(solution)/shard_map/ppermute | solution.py:27
  243.3 39.3 %collective-permute-start.1 = (bf16[2,1,1,2,384,384]{5,4,3,2,1,0:T(8,128)(2,1)}, bf16[2,1,1,2,384,384]{5,4,3,2,1,0:T(8,128)(2,1)S(1)}, u32[]{:S(2)}, u32[]{:S(2)}) collective-permute-start(bf16[2,1,1,2,384,384]{5,4,3,2,1,0:T(8,128)(2,1)} %param.16), channel_id=1, source_target_pairs={{64,0},{128,64},{192,128},{256,192},{320,256},{384,320},{448,384},... | collective-permute-start | bytes 3538952 | tf_op jit(solution)/shard_map/ppermute | solution.py:28
  282.8 92.0 %collective-permute-start.2 = (bf16[2,3,1,2,384,384]{5,4,3,2,1,0:T(8,128)(2,1)S(1)}, bf16[2,3,1,2,384,384]{5,4,3,2,1,0:T(8,128)(2,1)}, u32[]{:S(2)}, u32[]{:S(2)}) collective-permute-start(bf16[2,3,1,2,384,384]{5,4,3,2,1,0:T(8,128)(2,1)S(1)} %constant_dynamic-update-slice_fusion.2), channel_id=1, source_target_pairs={{0,8},{8,16},{16,24},{24,32},{32,40},{40,48},{48,56},{1,9},{9,17},... | collective-permute-start | bytes 10616840 | tf_op jit(solution)/shard_map/ppermute | solution.py:27
  285.9 172.4 %collective-permute-start.3 = (bf16[2,3,1,2,384,384]{5,4,3,2,1,0:T(8,128)(2,1)S(1)}, bf16[2,3,1,2,384,384]{5,4,3,2,1,0:T(8,128)(2,1)}, u32[]{:S(2)}, u32[]{:S(2)}) collective-permute-start(bf16[2,3,1,2,384,384]{5,4,3,2,1,0:T(8,128)(2,1)S(1)} %constant_dynamic-update-slice_fusion.2), channel_id=1, source_target_pairs={{8,0},{16,8},{24,16},{32,24},{40,32},{48,40},{56,48},{9,1},{17,9},... | collective-permute-start | bytes 10616840 | tf_op jit(solution)/shard_map/ppermute | solution.py:28
  492.5 5.4 copy-start.2
  492.5 5.4 copy-start.4
  497.9 10.3 %copy-start = (f32[3584]{0:T(1024)S(1)}, f32[3584]{0:T(1024)}, u32[]{:S(2)}) copy-start(f32[3584]{0:T(1024)} %concatenate.27) | copy-start | bytes 43012
  528.2 0.7 copy-start.3
  529.0 21.4 %copy-start.9 = (f32[3,128]{1,0:T(4,128)S(1)}, f32[3,128]{1,0:T(4,128)}, u32[]{:S(2)}) copy-start(f32[3,128]{1,0:T(4,128)} %copy-done.8) | copy-start | bytes 4612
  529.0 143.6 %copy-start.7 = (f32[3,128]{1,0:T(4,128)S(1)}, f32[3,128]{1,0:T(4,128)}, u32[]{:S(2)}) copy-start(f32[3,128]{1,0:T(4,128)} %copy-done.6) | copy-start | bytes 4612
  809.2 75.9 %copy-start.5 = (f32[3,128,128]{1,2,0:T(8,128)S(1)}, f32[3,128,128]{1,2,0:T(8,128)}, u32[]{:S(2)}) copy-start(f32[3,128,128]{1,2,0:T(8,128)} %get-tuple-element.350) | copy-start | bytes 589828
Sparse Core Ops, SparseCore 0:
  10.7 212.4 all-gather.8
  240.9 317.7 all-gather.10
